TPU v7x, 32 devices: a whole 2x2x4 slice. The times are simulated.
32 devices in a mesh: row: 4 (over y, x), col: 8 (over z, core).
Axes of the slice: x: 2, y: 2, z: 4, core: 2. Of those that a mesh axis runs over, the one named last changes fastest.
Arguments:
- vectors: bfloat16 [512, 8192], P('row', 'col'), may hold values from -6 to 6
- factor_tiles: bfloat16 [32, 24, 256, 256], P('row', 'col'), may hold values from -0.109375 to 0.109375
- tile_columns: int32 [32, 24], P('row', 'col'), may hold values from 0 to 31, as said below
- live_counts: int32 [32, 8], P('row', 'col'), may hold values from 0 to 3, as said below
Outputs:
- applied: float32 [512, 8192], P('row', 'col')
Inputs may be any that keep to these rules, and one draw needn't show every extreme that they name: `tile_columns`: slot s holds a tile column in [(s // 3) * 4, (s // 3 + 1) * 4); the slots of one row tile name distinct columns; a live slot's column is at most its row tile; the row tile's own column is always live, in the first slot of its group. `live_counts`: counts never exceed the columns allowed in that group, so the upper right region of groups is empty. In group 0 every row tile i >= 2 has exactly 3 live slots.
All inputs are finite; a program needn't handle non-finite values.
Results may differ from a plain program's by a relative error of at most 0.002.
Values may be sent and summed in bfloat16 or wider, within the bound.
A program may use at most 64 MiB of HBM per device.

v0:
```python
import jax
import jax.numpy as jnp
from jax import lax
from jax.sharding import PartitionSpec as P


def per_device(vectors, factor_tiles, tile_columns, live_counts):
    row_tiles = factor_tiles.shape[0]
    slot_count = factor_tiles.shape[1]
    tile_size = factor_tiles.shape[2]
    col_tiles = vectors.shape[1] // tile_size
    offset = lax.axis_index("col") * col_tiles
    local_cols = tile_columns - offset
    slot_index = lax.broadcasted_iota(jnp.int32, (row_tiles, slot_count), 1)
    live_mask = (slot_index < live_counts).astype(jnp.float32)
    column_iota = lax.broadcasted_iota(jnp.int32, (row_tiles, slot_count, col_tiles), 2)
    select_map = (local_cols[:, :, None] == column_iota).astype(jnp.float32) * live_mask[:, :, None]
    select_half = select_map.astype(jnp.bfloat16)
    vector_rows = lax.all_gather(vectors, "row", axis=0, tiled=True)
    count_rows = vector_rows.shape[0]
    blocks = vector_rows.reshape(count_rows, col_tiles, tile_size)
    picked = jnp.einsum(
        "tkj,vjc->tkvc", select_half, blocks, preferred_element_type=jnp.float32
    ).astype(jnp.bfloat16)
    partial_value = jnp.einsum(
        "tkab,tkvb->vta", factor_tiles, picked, preferred_element_type=jnp.float32
    )
    partial_all = partial_value.reshape(count_rows, row_tiles * tile_size)
    rowvals = lax.psum(partial_all, "col").astype(jnp.bfloat16)
    count_rows = rowvals.shape[0]
    weights = rowvals.reshape(count_rows, row_tiles, tile_size)
    contrib = jnp.einsum(
        "tkab,vta->tkvb", factor_tiles, weights, preferred_element_type=jnp.float32
    )
    summed = jnp.einsum("tkj,tkvb->vjb", select_map, contrib, precision=lax.Precision.HIGHEST)
    return lax.psum_scatter(
        summed.reshape(count_rows, col_tiles * tile_size), "row", scatter_dimension=0, tiled=True
    )


def solution(mesh):
    in_specs = (P("row", "col"), P("row", "col", None, None), P("row", "col"), P("row", "col"))
    out_specs = P("row", "col")
    return jax.shard_map(
        per_device, mesh=mesh, in_specs=in_specs, out_specs=out_specs, check_vma=False
    )
```

profile of v0, /device:TPU:0, one launch (start us, length us, event | category | flops | bytes accessed | tf_op | source)
XLA Modules:
  0.0 195.0 jit_solution(5123145907293766464)
XLA Ops:
  6.5 0.0 copy-start
  6.5 0.0 all-gather.2.cloned.1.call-start
  6.5 0.7 all-gather.2.cloned.1.call-update
  7.3 0.0 reduce-scatter.2.cloned.1.call-start
  7.3 0.8 fusion.13
  8.1 0.7 broadcast_subtract_fusion
  8.8 29.6 %all-gather.2.cloned.1.call-done = bf16[512,1024]{1,0:T(8,128)(2,1)} async-done(((bf16[128,1024]{1,0:T(8,128)(2,1)}), bf16[512,1024]{1,0:T(8,128)(2,1)}) %all-gather.2.cloned.1.call-update) | async-done | bytes 1048592 | tf_op jit(solution)/shard_map/all_gather | solution.py:19
  38.4 2.6 %reshape.39 = bf16[512,4,256,1]{2,1,0,3:T(4,128)(2,1)} reshape(bf16[512,1024]{1,0:T(8,128)(2,1)} %all-gather.2.cloned.1.call-done) | data formatting | bytes 2097152 | tf_op jit(solution)/shard_map/reshape | solution.py:21
  41.1 3.5 %fusion.5 = bf16[8,3,512,256]{3,0,2,1:T(8,128)(2,1)S(1)} fusion(bf16[512,4,256,1]{2,1,0,3:T(4,128)(2,1)} %reshape.39, f32[8,3]{0,1:T(4,128)S(1)} %fusion.13, s32[8,3]{0,1:T(4,128)S(1)} %broadcast_subtract_fusion), kind=kOutput, calls=%fused_computation.9 | convolution fusion | flops 25166016 | bytes 7340224 | tf_op jit(solution)/shard_map/tkj,vjc->tkvc/dot_general | solution.py:22
  44.6 0.0 copy-done
  44.6 4.1 %fusion.3 = f32[8,512,256,1]{1,2,3,0:T(8,128)} fusion(bf16[8,3,256,256]{3,2,1,0:T(8,128)(2,1)S(1)} %copy-done, bf16[8,3,512,256]{3,0,2,1:T(8,128)(2,1)S(1)} %fusion.5), kind=kOutput, calls=%fused_computation.4 | convolution fusion | flops 1610612736 | bytes 13631488 | tf_op jit(solution)/shard_map/tkab,tkvb->vta/dot_general | solution.py:25
  48.7 89.4 %all-reduce.1 = bf16[512,2048]{0,1:T(8,128)(2,1)} all-reduce(f32[512,2048]{0,1:T(8,128)} %bitcast.33), channel_id=1, replica_groups=mesh['row'=4,'col'=8] {'col'}, use_global_device_ids=true, to_apply=%region_0.0 | all-reduce | flops 1048576 | bytes 6291456 | tf_op jit(solution)/shard_map/psum | solution.py:29
  138.1 3.4 %fusion.16 = f32[8,512,3,256]{3,1,2,0:T(8,128)S(1)} fusion(bf16[512,8,256,1]{0,2,3,1:T(8,128)(2,1)} %bitcast.34, bf16[8,3,256,256]{3,2,1,0:T(8,128)(2,1)S(1)} %copy-done), kind=kOutput, calls=%fused_computation.21 | convolution fusion | flops 1610612736 | bytes 17825792 | tf_op jit(solution)/shard_map/tkab,vta->tkvb/dot_general | solution.py:32
  141.5 11.5 %fusion = f32[512,256,4,1]{1,2,3,0:T(4,128)S(1)} fusion(f32[8,512,3,256]{3,1,2,0:T(8,128)S(1)} %fusion.16, f32[8,3]{0,1:T(4,128)S(1)} %fusion.13, s32[8,3]{0,1:T(4,128)S(1)} %broadcast_subtract_fusion), kind=kOutput, calls=%fused_computation | convolution fusion | flops 150995136 | bytes 14680256 | tf_op jit(solution)/shard_map/tkj,tkvb->vjb/dot_general | solution.py:35
  153.0 1.8 copy.11
  154.8 0.0 reduce-scatter.2.cloned.1.call-update
  154.9 33.3 %reduce-scatter.2.cloned.1.call-done = f32[128,1024]{1,0:T(8,128)} async-done(((f32[512,1024]{1,0:T(8,128)}), f32[128,1024]{1,0:T(8,128)}) %reduce-scatter.2.cloned.1.call-update) | async-done | bytes 524304 | tf_op jit(solution)/shard_map/reduce_scatter | solution.py:36
Async XLA Ops:
  6.5 38.1 %copy-start = (bf16[8,3,256,256]{3,2,1,0:T(8,128)(2,1)S(1)}, bf16[8,3,256,256]{3,2,1,0:T(8,128)(2,1)}, u32[]{:S(2)}) copy-start(bf16[8,3,256,256]{3,2,1,0:T(8,128)(2,1)} %param.5) | copy-start | bytes 9437188
  6.5 31.9 %all-gather.2.cloned.1.call-start = ((), (), s32[]{:S(2)}) async-start(), calls=%async_computation.1 | async-start | bytes 1310720 | tf_op jit(solution)/shard_map/all_gather | solution.py:19
  7.3 180.9 %reduce-scatter.2.cloned.1.call-start = ((), (), s32[]{:S(2)}) async-start(), calls=%async_computation.2 | async-start | bytes 2621440 | tf_op jit(solution)/shard_map/reduce_scatter | solution.py:36
Sparse Core Ops, SparseCore 0:
  9.2 29.2 all-gather.1
  155.0 33.1 reduce-scatter.1
where the time goes:
time: 195 us
  blocking collectives  89.4 us (46%)
  waiting for transfers between devices  63.7 us (33%)
  matrix products  22.5 us (12%)
  between operations  13.4 us (7%)
  local copies, waits for them, and re-layouts  4.45 us (2%)
    psum x1, blocking collectives, per_device(): rowvals = lax.psum(partial_all, 'col').astype(jnp.bfloat16)  89.4 us
    reduce_scatter x1, waiting for transfers between devices, per_device(): lax.psum_scatter(summed.reshape(count_rows, col_tiles * tile_size), 'row'...  33.3 us
    all_gather x1, waiting for transfers between devices, per_device(): vector_rows = lax.all_gather(vectors, 'row', axis=0, tiled=True)  29.6 us
    dot_general x1, matrix products, per_device(): jnp.einsum('tkj,tkvb->vjb', select_map, contrib, precision=lax.Precision....  11.5 us
    dot_general x1, matrix products, per_device(): jnp.einsum('tkab,tkvb->vta', factor_tiles, picked, preferred_element_type...  4.12 us
  transfers between devices with their start and end apart: 2, of which 2 were waited for; matrix products, arithmetic and copies ran while one was open for 1% of the time, Pallas kernels for 0%

commit v1 on v0

--- a/solution.py
+++ b/solution.py
@@ -26,7 +26,7 @@
         "tkab,tkvb->vta", factor_tiles, picked, preferred_element_type=jnp.float32
     )
     partial_all = partial_value.reshape(count_rows, row_tiles * tile_size)
-    rowvals = lax.psum(partial_all, "col").astype(jnp.bfloat16)
+    rowvals = jnp.sum(lax.all_gather(partial_all, "col"), axis=0).astype(jnp.bfloat16)
     count_rows = rowvals.shape[0]
     weights = rowvals.reshape(count_rows, row_tiles, tile_size)
     contrib = jnp.einsum(

time: 195 us -> 418 us (2.14)
  waiting for transfers between devices: 63.7 us -> 352 us
  blocking collectives: 89.4 us -> 0 us
  other arithmetic: 1.51 us -> 15.2 us
  local copies, waits for them, and re-layouts: 4.45 us -> 13.8 us
    all_gather x0 -> x1, waiting for transfers between devices: none -> 289 us  [per_device(): lax.all_gather(partial_all, 'col')]
    psum x1 -> x0, blocking collectives: 89.4 us -> none  [per_device(): rowvals = lax.psum(partial_all, 'col').astype(jnp.bfloat16)]
    reduce_sum x0 -> x1, other arithmetic: none -> 13.7 us  [per_device(): jnp.sum(lax.all_gather(partial_all, 'col'), axis=0).astype(jnp.bfloat16)]
    another operation x0 -> x1, local copies, waits for them, and re-layouts: none -> 5.45 us  [per_device(): lax.all_gather(partial_all, 'col')]
  transfers between devices with their start and end apart: 2 -> 3, of which waited for: 2 -> 3; matrix products, arithmetic and copies ran while one was open for 1% -> 0% of each run, Pallas kernels for 0% -> 0%
where the time goes in v1:
time: 418 us; the launch traced here: 417 us
  waiting for transfers between devices  352 us (84%)
  matrix products  22.5 us (5%)
  other arithmetic  15.2 us (4%)
  local copies, waits for them, and re-layouts  13.8 us (3%)
  between operations  13.1 us (3%)
    all_gather x1, waiting for transfers between devices, per_device(): lax.all_gather(partial_all, 'col')  289 us
    reduce_scatter x1, waiting for transfers between devices, per_device(): lax.psum_scatter(summed.reshape(count_rows, col_tiles * tile_size), 'row'...  33.5 us
    all_gather x1, waiting for transfers between devices, per_device(): vector_rows = lax.all_gather(vectors, 'row', axis=0, tiled=True)  29.6 us
    reduce_sum x1, other arithmetic, per_device(): jnp.sum(lax.all_gather(partial_all, 'col'), axis=0).astype(jnp.bfloat16)  13.7 us
    dot_general x1, matrix products, per_device(): jnp.einsum('tkj,tkvb->vjb', select_map, contrib, precision=lax.Precision....  11.5 us
  transfers between devices with their start and end apart: 3, of which 3 were waited for; matrix products, arithmetic and copies ran while one was open for 0% of the time, Pallas kernels for 0%

profile of v1, /device:TPU:0, one launch (start us, length us, event | category | flops | bytes accessed | tf_op | source)
XLA Modules:
  0.0 417.3 jit_solution(15544819288021617217)
XLA Ops:
  6.5 0.0 copy-start
  6.5 0.0 all-gather.3.cloned.1.call-start
  6.5 0.7 all-gather.3.cloned.1.call-update
  7.3 0.0 all-gather.5.cloned.1.call-start
  7.3 0.8 fusion.13
  8.1 0.7 broadcast_subtract_fusion
  8.8 29.6 %all-gather.3.cloned.1.call-done = bf16[512,1024]{1,0:T(8,128)(2,1)} async-done(((bf16[128,1024]{1,0:T(8,128)(2,1)}), bf16[512,1024]{1,0:T(8,128)(2,1)}) %all-gather.3.cloned.1.call-update) | async-done | bytes 1048592 | tf_op jit(solution)/shard_map/all_gather | solution.py:19
  38.4 2.6 reshape.34
  41.1 3.5 fusion.5
  44.6 0.0 copy-done
  44.6 4.1 fusion.3
  48.7 5.4 %copy.5 = f32[1,512,2048]{2,1,0:T(8,128)} copy(f32[1,512,2048]{1,2,0:T(8,128)} %bitcast.33) | data formatting | bytes 8388608 | tf_op jit(solution)/shard_map/all_gather;reshape | solution.py:29
  54.2 0.0 all-gather.5.cloned.1.call-update
  54.2 0.2 reduce-scatter.2.cloned.1.call-start
  54.4 288.5 %all-gather.5.cloned.1.call-done = f32[8,512,2048]{2,1,0:T(8,128)} async-done(((f32[1,512,2048]{2,1,0:T(8,128)}), f32[8,512,2048]{2,1,0:T(8,128)}) %all-gather.5.cloned.1.call-update) | async-done | bytes 33554448 | tf_op jit(solution)/shard_map/all_gather | solution.py:29
  342.9 13.7 %reduce_sum.9 = bf16[512,2048]{1,0:T(8,128)(2,1)} reduce(f32[8,512,2048]{2,1,0:T(8,128)} %all-gather.5.cloned.1.call-done, f32[]{:T(128)} %constant.8.clone.1), dimensions={0}, to_apply=%region_0.0 | reduce | flops 7340032 | bytes 35651588 | tf_op jit(solution)/shard_map/reduce_sum | solution.py:29
  356.6 3.9 copy.13
  360.5 3.4 fusion.16
  363.9 11.5 %fusion = f32[512,256,4,1]{1,2,3,0:T(4,128)S(1)} fusion(f32[8,512,3,256]{3,1,2,0:T(8,128)S(1)} %fusion.16, f32[8,3]{0,1:T(4,128)S(1)} %fusion.13, s32[8,3]{0,1:T(4,128)S(1)} %broadcast_subtract_fusion), kind=kOutput, calls=%fused_computation | convolution fusion | flops 150995136 | bytes 14680256 | tf_op jit(solution)/shard_map/tkj,tkvb->vjb/dot_general | solution.py:35
  375.4 1.8 copy.14
  377.2 0.0 reduce-scatter.2.cloned.1.call-update
  377.3 33.5 %reduce-scatter.2.cloned.1.call-done = f32[128,1024]{1,0:T(8,128)} async-done(((f32[512,1024]{1,0:T(8,128)}), f32[128,1024]{1,0:T(8,128)}) %reduce-scatter.2.cloned.1.call-update) | async-done | bytes 524304 | tf_op jit(solution)/shard_map/reduce_scatter | solution.py:36
Async XLA Ops:
  6.5 38.0 %copy-start = (bf16[8,3,256,256]{3,2,1,0:T(8,128)(2,1)S(1)}, bf16[8,3,256,256]{3,2,1,0:T(8,128)(2,1)}, u32[]{:S(2)}) copy-start(bf16[8,3,256,256]{3,2,1,0:T(8,128)(2,1)} %param.5) | copy-start | bytes 9437188
  6.5 31.9 %all-gather.3.cloned.1.call-start = ((), (), s32[]{:S(2)}) async-start(), calls=%async_computation.1 | async-start | bytes 1310720 | tf_op jit(solution)/shard_map/all_gather | solution.py:19
  7.3 335.7 %all-gather.5.cloned.1.call-start = ((), (), s32[]{:S(2)}) async-start(), calls=%async_computation.2 | async-start | bytes 37748736 | tf_op jit(solution)/shard_map/all_gather | solution.py:29
  54.2 356.6 %reduce-scatter.2.cloned.1.call-start = ((), (), s32[]{:S(2)}) async-start(), calls=%async_computation.3 | async-start | bytes 2621440 | tf_op jit(solution)/shard_map/reduce_scatter | solution.py:36
Sparse Core Ops, SparseCore 0:
  9.2 29.2 all-gather.2
  54.3 288.5 all-gather.4
  377.4 33.3 reduce-scatter.1
